TPU v7x, 32 devices: a whole 2x2x4 slice. The times are simulated.
32 devices in a mesh: col: 16 (over z, x, core), tok: 2 (over y).
Axes of the slice: x: 2, y: 2, z: 4, core: 2. Of those that a mesh axis runs over, the one named last changes fastest.
Arguments:
- acts: bfloat16 [512, 8192], P('tok', 'col'), may hold values from -6 to 6
- grad_out: bfloat16 [512, 8192], P('tok', 'col'), may hold values from -0.19921875 to 0.19921875
- left_factor: float32 [8, 8192, 1024], P('tok', 'col'), may hold values from -6 to 6
- right_factor: float32 [8, 8192, 1024], P('tok', 'col'), may hold values from -6 to 6
- left_basis: bfloat16 [8, 8192, 1024], P('tok', 'col'), may hold values from -0.1875 to 0.1875
- right_basis: bfloat16 [8, 8192, 1024], P('tok', 'col'), may hold values from -0.1875 to 0.1875
- moment: float32 [8192, 8192], P('tok', 'col'), may hold values from -2 to 2
- second: float32 [8192, 8192], P('tok', 'col'), may hold values from 0.05 to 2
Outputs:
- left_out: float32 [8, 8192, 1024], P('tok', 'col')
- right_out: float32 [8, 8192, 1024], P('tok', 'col')
- moment_out: float32 [8192, 8192], P('tok', 'col')
- second_out: float32 [8192, 8192], P('tok', 'col')
- update: bfloat16 [8192, 8192], P('tok', 'col')
All inputs are finite; a program needn't handle non-finite values.
Results may differ from a plain program's by a relative error of at most 0.0075.
Values may be sent and summed in bfloat16 or wider, within the bound.
No kernel may reach another device: no remote copies, remote signals or barrier semaphores. Data moves between devices by JAX's collectives and lax.ppermute only.
A program may use at most 192 MiB of HBM per device.

v0:
```python
import jax
import jax.numpy as jnp
from jax import lax
from jax.sharding import PartitionSpec as P

B = 1024
shampoo_beta = 0.95
first_beta = 0.9
second_beta = 0.95
first_corr = 1.0 - 0.9**4
second_corr = 1.0 - 0.95**4
epsilon = 1e-08


def swapped(array, axis, distance):
    return lax.ppermute(array, axis, [(i, i ^ 1 << distance) for i in range(lax.axis_size(axis))])


def join_pair(current, incoming, axis, lower):
    width = current.shape[axis]
    shape = list(current.shape)
    shape[axis] = 2 * width
    joined = jnp.zeros(shape, current.dtype)
    mine_at = jnp.where(lower, 0, width)
    theirs_at = width - mine_at
    joined = lax.dynamic_update_slice_in_dim(joined, current, mine_at, axis)
    return lax.dynamic_update_slice_in_dim(joined, incoming, theirs_at, axis)


def shards(acts, grad_out, left_factor, right_factor, left_basis, right_basis, moment, second):
    width = grad_out.shape[1]
    blocks = left_factor.shape[0]
    groups = B // width
    nbits = groups.bit_length() - 1
    member = lax.axis_index("col") % groups
    contract = (((0,), (0,)), ((), ()))
    whole = lax.all_gather(acts, "col", axis=1, tiled=True)
    block_rows = lax.all_to_all(whole, "tok", split_axis=1, concat_axis=0, tiled=True)
    all_grads = lax.all_gather(grad_out, "tok", axis=0, tiled=True)
    grad = lax.dot_general(block_rows, all_grads, contract, preferred_element_type=jnp.float32)
    own = grad.astype(jnp.bfloat16).reshape(blocks, B, width)
    tiles, left_full, right_full = (own, left_basis, right_basis)
    for bit in range(nbits):
        other = swapped((tiles, left_full, right_full), "col", bit)
        lower = member >> bit & 1 == 0
        tiles = join_pair(tiles, other[0], 2, lower)
        left_full = join_pair(left_full, other[1], 1, lower)
        right_full = join_pair(right_full, other[2], 1, lower)
    right_cols = lax.dynamic_slice_in_dim(right_full, member * width, width, 2)
    mixed = jnp.einsum(
        "nab,nbc->nac", tiles, right_cols, preferred_element_type=jnp.float32
    ).astype(jnp.bfloat16)
    lead = lax.dynamic_slice_in_dim(tiles, member * width, width, 1)
    left_new = shampoo_beta * left_factor + (1.0 - shampoo_beta) * jnp.einsum(
        "nab,ncb->nac", lead, tiles, preferred_element_type=jnp.float32
    )
    right_new = shampoo_beta * right_factor + (1.0 - shampoo_beta) * jnp.einsum(
        "nat,nab->ntb", own, tiles, preferred_element_type=jnp.float32
    )
    rotated = jnp.einsum("nab,nac->nbc", left_full, mixed, preferred_element_type=jnp.float32)
    first_new = first_beta * moment.reshape(blocks, B, width) + (1.0 - first_beta) * rotated
    second_new = (
        second_beta * second.reshape(blocks, B, width) + (1.0 - second_beta) * rotated * rotated
    )
    normed = (first_new / first_corr / (jnp.sqrt(second_new / second_corr) + epsilon)).astype(
        jnp.bfloat16
    )
    steps_full = normed
    for bit in range(nbits):
        other_steps = swapped(steps_full, "col", bit)
        lower = member >> bit & 1 == 0
        steps_full = join_pair(steps_full, other_steps, 2, lower)
    back = jnp.einsum(
        "nab,ncb->nac", steps_full, right_basis, preferred_element_type=jnp.float32
    ).astype(jnp.bfloat16)
    update = jnp.einsum("nab,nbc->nac", left_full, back, preferred_element_type=jnp.float32).astype(
        jnp.bfloat16
    )
    rows = blocks * B
    return (
        left_new,
        right_new,
        first_new.reshape(rows, width),
        second_new.reshape(rows, width),
        update.reshape(rows, width),
    )


def solution(mesh):
    in_specs = (
        P("tok", "col"),
        P("tok", "col"),
        P("tok", "col", None),
        P("tok", "col", None),
        P("tok", "col", None),
        P("tok", "col", None),
        P("tok", "col"),
        P("tok", "col"),
    )
    out_specs = (
        P("tok", "col", None),
        P("tok", "col", None),
        P("tok", "col"),
        P("tok", "col"),
        P("tok", "col"),
    )
    return jax.shard_map(shards, mesh=mesh, in_specs=in_specs, out_specs=out_specs, check_vma=False)
```

profile of v0, /device:TPU:0, one launch (start us, length us, event | category | flops | bytes accessed | tf_op | source)
XLA Modules:
  0.0 273.9 jit_solution(15779307181880031778)
XLA Ops:
  7.2 1.8 copy.17
  9.1 54.8 %all-gather.2.cloned.1.call-done = bf16[256,8192]{0,1:T(8,128)(2,1)} async-done(((bf16[256,512]{0,1:T(8,128)(2,1)}), bf16[256,8192]{0,1:T(8,128)(2,1)}) %all-gather.2.cloned.1.call-update) | async-done | bytes 4194320 | tf_op jit(solution)/shard_map/all_gather | solution.py:37
  63.8 5.6 %all-to-all-start = ((bf16[256,2,4096]{0,2,1:T(8,128)(2,1)}), bf16[256,2,4096]{0,2,1:T(8,128)(2,1)}, u32[]{:S(2)}, u32[]{:S(2)}) async-start(bf16[256,2,4096]{0,2,1:T(8,128)(2,1)} %bitcast.34), calls=%async_computation | async-start | bytes 8388608 | tf_op jit(solution)/shard_map/all_to_all | solution.py:38
  70.0 53.0 %all_gather.7 = bf16[512,512]{1,0:T(8,128)(2,1)S(1)} all-gather(bf16[256,512]{1,0:T(8,128)(2,1)S(1)} %copy-done.2), channel_id=1, replica_groups=mesh['col'=16,'tok'=2] {'tok'}, dimensions={0}, use_global_device_ids=true | all-gather | bytes 786432 | tf_op jit(solution)/shard_map/all_gather | solution.py:39
  123.1 6.3 %copy.18 = bf16[2,256,4096]{2,1,0:T(8,128)(2,1)} copy(bf16[2,256,4096]{1,2,0:T(8,128)(2,1)} %bitcast.1) | data formatting | bytes 8388608 | tf_op jit(solution)/shard_map/all_to_all | solution.py:38
  129.4 6.5 %convolution_convert_fusion = bf16[4096,512]{1,0:T(8,128)(2,1)} fusion(bf16[512,4096]{1,0:T(8,128)(2,1)} %bitcast.35, bf16[512,512]{1,0:T(8,128)(2,1)S(1)} %all_gather.7), kind=kOutput, calls=%fused_computation.6 | convolution fusion | flops 2149580800 | bytes 8912896 | tf_op jit(solution)/shard_map/dot_general | solution.py:40
  135.9 4.5 %broadcast.17.clone.2 = bf16[4,1024,1024]{2,1,0:T(8,128)(2,1)} broadcast(bf16[]{:T(256)} %constant.17.clone.1), dimensions={} | broadcast | bytes 8388610 | tf_op jit(solution)/shard_map/broadcast.5
  140.4 2.6 constant_dynamic-update-slice_fusion.3
  143.0 4.3 %broadcast.17.clone.1 = bf16[4,1024,1024]{2,1,0:T(8,128)(2,1)} broadcast(bf16[]{:T(256)} %constant.17.clone.1), dimensions={} | broadcast | bytes 8388610 | tf_op jit(solution)/shard_map/broadcast.5
  147.3 2.6 constant_dynamic-update-slice_fusion.5
  149.9 1.1 slice-done.1
  151.0 4.5 %broadcast_multiply_fusion.1 = f32[4096,512]{1,0:T(8,128)} fusion(f32[4096,512]{1,0:T(8,128)S(1)} %bitcast.29), kind=kLoop, calls=%fused_computation.14 | loop fusion | flops 2097152 | bytes 16777216 | tf_op jit(solution)/shard_map/mul | solution.py:61
  155.5 4.5 %broadcast_multiply_fusion = f32[4096,512]{1,0:T(8,128)} fusion(f32[4096,512]{1,0:T(8,128)S(1)} %bitcast.31), kind=kLoop, calls=%fused_computation.9 | loop fusion | flops 2097152 | bytes 16777216 | tf_op jit(solution)/shard_map/mul | solution.py:63
  160.0 4.6 %constant_dynamic-update-slice_fusion.2 = bf16[4,1024,1024]{2,1,0:T(8,128)(2,1)} fusion(bf16[4,1024,1024]{2,1,0:T(8,128)(2,1)} %constant_dynamic-update-slice_fusion.3, bf16[4,512,1024]{2,1,0:T(8,128)(2,1)} %collective-permute-done.2, s32[]{:T(128)S(6)} %select_n.30), kind=kLoop, calls=%fused_computation.21 | loop fusion | bytes 8388612 | tf_op jit(solution)/shard_map/dynamic_update_slice | solution.py:27
  164.6 4.7 %constant_dynamic-update-slice_fusion.4 = bf16[4,1024,1024]{2,1,0:T(8,128)(2,1)} fusion(bf16[4,1024,1024]{2,1,0:T(8,128)(2,1)} %constant_dynamic-update-slice_fusion.5, bf16[4,512,1024]{2,1,0:T(8,128)(2,1)} %collective-permute-done.1, s32[]{:T(128)S(6)} %select_n.30), kind=kLoop, calls=%fused_computation.23 | loop fusion | bytes 8388612 | tf_op jit(solution)/shard_map/dynamic_update_slice | solution.py:27
  169.3 4.3 %broadcast.17.clone = bf16[4,1024,1024]{2,1,0:T(8,128)(2,1)} broadcast(bf16[]{:T(256)} %constant.17.clone.1), dimensions={} | broadcast | bytes 8388610 | tf_op jit(solution)/shard_map/broadcast.5
  173.6 4.6 %constant_dynamic-update-slice_fusion.7 = bf16[4,1024,1024]{2,1,0:T(8,128)(2,1)} fusion(bf16[4,1024,1024]{2,1,0:T(8,128)(2,1)} %broadcast.17.clone, bf16[4,1024,512]{2,1,0:T(8,128)(2,1)} %bitcast.3, s32[]{:T(128)S(6)} %select_n.29), kind=kLoop, calls=%fused_computation.27 | loop fusion | bytes 8388612 | tf_op jit(solution)/shard_map/dynamic_update_slice | solution.py:26
  178.2 4.5 %constant_dynamic-update-slice_fusion.6 = bf16[4,1024,1024]{2,1,0:T(8,128)(2,1)} fusion(bf16[4,1024,1024]{2,1,0:T(8,128)(2,1)} %constant_dynamic-update-slice_fusion.7, bf16[4,1024,512]{2,1,0:T(8,128)(2,1)} %collective-permute-done, s32[]{:T(128)S(6)} %select_n.30), kind=kLoop, calls=%fused_computation.26 | loop fusion | bytes 8388612 | tf_op jit(solution)/shard_map/dynamic_update_slice | solution.py:27
  182.7 4.3 %broadcast.17 = bf16[4,1024,1024]{2,1,0:T(8,128)(2,1)} broadcast(bf16[]{:T(256)} %constant.17.clone.1), dimensions={} | broadcast | bytes 8388610 | tf_op jit(solution)/shard_map/broadcast.5
  187.0 29.9 %constant_dynamic-update-slice_fusion.1 = (bf16[4,1024,1024]{2,1,0:T(8,128)(2,1)}, bf16[4,1024,512]{2,1,0:T(8,128)(2,1)}, f32[4,1024,512]{2,1,0:T(8,128)}, f32[4,1024,512]{2,1,0:T(8,128)}) fusion(bf16[4,1024,1024]{2,1,0:T(8,128)(2,1)} %broadcast.17, s32[]{:T(128)S(6)} %select_n.29, f32[4,1024,512]{2,1,0:T(8,128)} %bitcast.33, f32[4,1024,512]{2,1,0:T(8,128)} %bitcast.32, ...), kind=kOutput, calls=%fused_computation.19 | convolution fusion | flops 8613003264 | bytes 62914568 | tf_op jit(solution)/shard_map/nab,nac->nbc/dot_general | solution.py:60
  217.3 15.4 %multiply_add_fusion.2 = f32[4,512,1024]{2,1,0:T(8,128)} fusion(f32[4,512,1024]{2,1,0:T(8,128)} %param.10, bf16[4,1024,1024]{2,1,0:T(8,128)(2,1)} %constant_dynamic-update-slice_fusion.6, s32[]{:T(128)S(6)} %select_n.31), kind=kOutput, calls=%fused_computation.5 | convolution fusion | flops 4301258752 | bytes 29360132 | tf_op jit(solution)/shard_map/nab,ncb->nac/dot_general | solution.py:54
  232.8 15.3 %multiply_add_fusion.1 = f32[4,512,1024]{2,1,0:T(8,128)} fusion(f32[4,512,1024]{2,1,0:T(8,128)} %param.11, bf16[4,1024,512]{2,1,0:T(8,128)(2,1)} %bitcast.3, bf16[4,1024,1024]{2,1,0:T(8,128)(2,1)} %constant_dynamic-update-slice_fusion.6), kind=kOutput, calls=%fused_computation.4 | convolution fusion | flops 4301258752 | bytes 29360128 | tf_op jit(solution)/shard_map/nat,nab->ntb/dot_general | solution.py:57
  248.1 4.5 %constant_dynamic-update-slice_fusion = bf16[4,1024,1024]{2,1,0:T(8,128)(2,1)} fusion(bf16[4,1024,1024]{2,1,0:T(8,128)(2,1)} %get-tuple-element.5, bf16[4,1024,512]{2,1,0:T(8,128)(2,1)} %collective-permute-done.3, s32[]{:T(128)S(6)} %select_n.30), kind=kLoop, calls=%fused_computation.18 | loop fusion | bytes 8388612 | tf_op jit(solution)/shard_map/dynamic_update_slice | solution.py:27
  252.6 14.5 %fusion.13 = bf16[4,1024,512]{2,1,0:T(8,128)(2,1)} fusion(bf16[4,1024,1024]{2,1,0:T(8,128)(2,1)} %constant_dynamic-update-slice_fusion.4, bf16[4,1024,1024]{2,1,0:T(8,128)(2,1)} %constant_dynamic-update-slice_fusion, bf16[4,512,1024]{2,1,0:T(8,128)(2,1)} %param.13), kind=kOutput, calls=%fused_computation.17 | convolution fusion | flops 8592031744 | bytes 25165824 | tf_op jit(solution)/shard_map/nab,nbc->nac/dot_general | solution.py:76
  (26 shorter events, 1.1 us)
Async XLA Ops:
  7.2 62.9 %copy-start.2 = (bf16[256,512]{1,0:T(8,128)(2,1)S(1)}, bf16[256,512]{1,0:T(8,128)(2,1)}, u32[]{:S(2)}) copy-start(bf16[256,512]{1,0:T(8,128)(2,1)} %param.9) | copy-start | bytes 786436
  7.2 56.7 %all-gather.2.cloned.1.call-start = ((), (), s32[]{:S(2)}) async-start(), calls=%async_computation.1 | async-start | bytes 4456448 | tf_op jit(solution)/shard_map/all_gather | solution.py:37
  63.8 59.2 %all-to-all-start = ((bf16[256,2,4096]{0,2,1:T(8,128)(2,1)}), bf16[256,2,4096]{0,2,1:T(8,128)(2,1)}, u32[]{:S(2)}, u32[]{:S(2)}) async-start(bf16[256,2,4096]{0,2,1:T(8,128)(2,1)} %bitcast.34), calls=%async_computation | async-start | bytes 8388608 | tf_op jit(solution)/shard_map/all_to_all | solution.py:38
  69.5 90.5 %collective-permute-start.2 = (bf16[4,512,1024]{2,1,0:T(8,128)(2,1)}, bf16[4,512,1024]{2,1,0:T(8,128)(2,1)}, u32[]{:S(2)}, u32[]{:S(2)}) collective-permute-start(bf16[4,512,1024]{2,1,0:T(8,128)(2,1)} %param.13), channel_id=1, source_target_pairs={{0,2},{2,0},{4,6},{6,4},{8,10},{10,8},{12,14},{14,12},{16,18},{18,... | collective-permute-start | bytes 12582920 | tf_op jit(solution)/shard_map/ppermute | solution.py:16
  69.8 94.8 %collective-permute-start.1 = (bf16[4,512,1024]{2,1,0:T(8,128)(2,1)}, bf16[4,512,1024]{2,1,0:T(8,128)(2,1)}, u32[]{:S(2)}, u32[]{:S(2)}) collective-permute-start(bf16[4,512,1024]{2,1,0:T(8,128)(2,1)} %param.12), channel_id=1, source_target_pairs={{0,2},{2,0},{4,6},{6,4},{8,10},{10,8},{12,14},{14,12},{16,18},{18,... | collective-permute-start | bytes 12582920 | tf_op jit(solution)/shard_map/ppermute | solution.py:16
  135.9 42.3 %collective-permute-start = (bf16[4,1024,512]{2,1,0:T(8,128)(2,1)}, bf16[4,1024,512]{2,1,0:T(8,128)(2,1)}, u32[]{:S(2)}, u32[]{:S(2)}) collective-permute-start(bf16[4,1024,512]{2,1,0:T(8,128)(2,1)} %bitcast.3), channel_id=1, source_target_pairs={{0,2},{2,0},{4,6},{6,4},{8,10},{10,8},{12,14},{14,12},{16,18},{18,... | collective-permute-start | bytes 12582920 | tf_op jit(solution)/shard_map/ppermute | solution.py:16
  135.9 4.5 %copy-start.1 = (bf16[4,512,1024]{2,1,0:T(8,128)(2,1)S(1)}, bf16[4,512,1024]{2,1,0:T(8,128)(2,1)}, u32[]{:S(2)}) copy-start(bf16[4,512,1024]{2,1,0:T(8,128)(2,1)} %param.13) | copy-start | bytes 12582916
  140.4 6.9 %copy-start = (bf16[4,512,1024]{2,1,0:T(8,128)(2,1)S(1)}, bf16[4,512,1024]{2,1,0:T(8,128)(2,1)}, u32[]{:S(2)}) copy-start(bf16[4,512,1024]{2,1,0:T(8,128)(2,1)} %param.12) | copy-start | bytes 12582916
  143.0 6.9 %slice-start = ((s8[8388608]{0:T(1024)(128)(4,1)}), s8[4194304]{0:T(1024)(128)(4,1)S(1)}, s32[]{:S(2)}) async-start(s8[8388608]{0:T(1024)(128)(4,1)} %bitcast.28), calls=%async_computation.2 | async-start | bytes 8388608
  147.3 3.7 %slice-start.1 = ((s8[8388608]{0:T(1024)(128)(4,1)}), s8[4194304]{0:T(1024)(128)(4,1)S(1)}, s32[]{:S(2)}) async-start(s8[8388608]{0:T(1024)(128)(4,1)} %bitcast.28), calls=%async_computation.3 | async-start | bytes 8388608
  147.3 8.2 %slice-start.2 = ((s8[8388608]{0:T(1024)(128)(4,1)}), s8[4194304]{0:T(1024)(128)(4,1)S(1)}, s32[]{:S(2)}) async-start(s8[8388608]{0:T(1024)(128)(4,1)} %bitcast.30), calls=%async_computation.4 | async-start | bytes 8388608
  151.0 4.5 %slice-start.3 = ((s8[8388608]{0:T(1024)(128)(4,1)}), s8[4194304]{0:T(1024)(128)(4,1)S(1)}, s32[]{:S(2)}) async-start(s8[8388608]{0:T(1024)(128)(4,1)} %bitcast.30), calls=%async_computation.5 | async-start | bytes 8388608
  216.9 31.2 %collective-permute-start.3 = (bf16[4,1024,512]{2,1,0:T(8,128)(2,1)}, bf16[4,1024,512]{2,1,0:T(8,128)(2,1)}, u32[]{:S(2)}, u32[]{:S(2)}) collective-permute-start(bf16[4,1024,512]{2,1,0:T(8,128)(2,1)} %get-tuple-element.6), channel_id=1, source_target_pairs={{0,2},{2,0},{4,6},{6,4},{8,10},{10,8},{12,14},{14,12},{16,18},{18,... | collective-permute-start | bytes 12582920 | tf_op jit(solution)/shard_map/ppermute | solution.py:16
Sparse Core Ops, SparseCore 0:
  10.7 53.0 all-gather.1
where the time goes:
time: 274 us
  matrix products  81.7 us (30%)
  waiting for transfers between devices  54.8 us (20%)
  local copies, waits for them, and re-layouts  54.7 us (20%)
  blocking collectives  53 us (19%)
  between operations  14.1 us (5%)
  other arithmetic  8.98 us (3%)
  starting transfers between devices  6.68 us (2%)
    all_gather x1, waiting for transfers between devices, shards(): whole = lax.all_gather(acts, 'col', axis=1, tiled=True)  54.8 us
    all_gather x1, blocking collectives, shards(): all_grads = lax.all_gather(grad_out, 'tok', axis=0, tiled=True)  53 us
    dot_general x1, matrix products, shards(): jnp.einsum('nab,nac->nbc', left_full, mixed, preferred_element_type=jnp.f...  29.9 us
    dynamic_update_slice x4, local copies, waits for them, and re-layouts, join_pair(): return lax.dynamic_update_slice_in_dim(joined, incoming, theirs_at, axis)  18.3 us
    another operation x4, local copies, waits for them, and re-layouts  17.4 us
    dot_general x1, matrix products, shards(): jnp.einsum('nab,ncb->nac', lead, tiles, preferred_element_type=jnp.float32)  15.4 us
    dot_general x1, matrix products, shards(): jnp.einsum('nat,nab->ntb', own, tiles, preferred_element_type=jnp.float32)  15.3 us
    dot_general x1, matrix products, shards(): jnp.einsum('nab,nbc->nac', left_full, back, preferred_element_type=jnp.fl...  14.5 us
  transfers between devices with their start and end apart: 6, of which 1 were waited for; matrix products, arithmetic and copies ran while one was open for 31% of the time, Pallas kernels for 0%

commit v1 on v0

--- a/solution.py
+++ b/solution.py
@@ -34,7 +34,12 @@
     nbits = groups.bit_length() - 1
     member = lax.axis_index("col") % groups
     contract = (((0,), (0,)), ((), ()))
-    whole = lax.all_gather(acts, "col", axis=1, tiled=True)
+    ring = [acts]
+    for hop in range(15):
+        ring.append(lax.ppermute(ring[-1], "col", [(dev, (dev + 1) % 16) for dev in range(16)]))
+    whole = jnp.roll(
+        jnp.concatenate(ring[::-1], axis=1), (lax.axis_index("col") + 1) * ring[0].shape[1], axis=1
+    )
     block_rows = lax.all_to_all(whole, "tok", split_axis=1, concat_axis=0, tiled=True)
     all_grads = lax.all_gather(grad_out, "tok", axis=0, tiled=True)
     grad = lax.dot_general(block_rows, all_grads, contract, preferred_element_type=jnp.float32)

time: 274 us -> 337 us (1.23)
  waiting for transfers between devices: 54.8 us -> 128 us
  between operations: 14.1 us -> 0.94 us
  local copies, waits for them, and re-layouts: 54.7 us -> 62.5 us
  blocking collectives: 53 us -> 46.1 us
    ppermute x0 -> x15, waiting for transfers between devices: none -> 128 us  [shards(): lax.ppermute(ring[-1], 'col', [(dev, (dev + 1) % 16) for dev in range(16)])]
    all_gather x1 -> x0, waiting for transfers between devices: 54.8 us -> none  [shards(): whole = lax.all_gather(acts, 'col', axis=1, tiled=True)]
    all_gather x1, blocking collectives: 53 us -> 46.1 us  [shards(): all_grads = lax.all_gather(grad_out, 'tok', axis=0, tiled=True)]
    unnamed x15 -> x50, local copies, waits for them, and re-layouts: 2.97 us -> 8.28 us
  transfers between devices with their start and end apart: 6 -> 20, of which waited for: 1 -> 15; matrix products, arithmetic and copies ran while one was open for 31% -> 25% of each run, Pallas kernels for 0% -> 0%
where the time goes in v1:
time: 337 us; the launch traced here: 336 us
  waiting for transfers between devices  128 us (38%)
  matrix products  81.7 us (24%)
  local copies, waits for them, and re-layouts  62.5 us (19%)
  blocking collectives  46.1 us (14%)
  other arithmetic  8.98 us (3%)
  starting transfers between devices  7.25 us (2%)
    ppermute x15, waiting for transfers between devices, shards(): lax.ppermute(ring[-1], 'col', [(dev, (dev + 1) % 16) for dev in range(16)])  128 us
    all_gather x1, blocking collectives, shards(): all_grads = lax.all_gather(grad_out, 'tok', axis=0, tiled=True)  46.1 us
    dot_general x1, matrix products, shards(): jnp.einsum('nab,nac->nbc', left_full, mixed, preferred_element_type=jnp.f...  29.9 us
    dynamic_update_slice x4, local copies, waits for them, and re-layouts, join_pair(): return lax.dynamic_update_slice_in_dim(joined, incoming, theirs_at, axis)  18.4 us
    another operation x4, local copies, waits for them, and re-layouts  17.5 us
    dot_general x1, matrix products, shards(): jnp.einsum('nab,ncb->nac', lead, tiles, preferred_element_type=jnp.float32)  15.4 us
    dot_general x1, matrix products, shards(): jnp.einsum('nat,nab->ntb', own, tiles, preferred_element_type=jnp.float32)  15.3 us
    dot_general x1, matrix products, shards(): jnp.einsum('nab,nbc->nac', left_full, back, preferred_element_type=jnp.fl...  14.5 us
  transfers between devices with their start and end apart: 20, of which 15 were waited for; matrix products, arithmetic and copies ran while one was open for 25% of the time, Pallas kernels for 0%

profile of v1, /device:TPU:0, one launch (start us, length us, event | category | flops | bytes accessed | tf_op | source)
XLA Modules:
  0.0 335.8 jit_solution(12581350725638169202)
XLA Ops:
  2.3 9.0 %collective-permute-done = bf16[256,512]{0,1:T(8,128)(2,1)S(1)} collective-permute-done((bf16[256,512]{0,1:T(8,128)(2,1)S(1)}, bf16[256,512]{0,1:T(8,128)(2,1)S(1)}, u32[]{:S(2)}, u32[]{:S(2)}) %collective-permute-start) | collective-permute-done | bytes 262176 | tf_op jit(solution)/shard_map/ppermute | solution.py:39
  11.3 8.5 %collective-permute-done.1 = bf16[256,512]{0,1:T(8,128)(2,1)S(1)} collective-permute-done((bf16[256,512]{0,1:T(8,128)(2,1)S(1)}, bf16[256,512]{0,1:T(8,128)(2,1)S(1)}, u32[]{:S(2)}, u32[]{:S(2)}) %collective-permute-start.1) | collective-permute-done | bytes 262176 | tf_op jit(solution)/shard_map/ppermute | solution.py:39
  19.8 8.5 %collective-permute-done.2 = bf16[256,512]{0,1:T(8,128)(2,1)S(1)} collective-permute-done((bf16[256,512]{0,1:T(8,128)(2,1)S(1)}, bf16[256,512]{0,1:T(8,128)(2,1)S(1)}, u32[]{:S(2)}, u32[]{:S(2)}) %collective-permute-start.2) | collective-permute-done | bytes 262176 | tf_op jit(solution)/shard_map/ppermute | solution.py:39
  28.3 8.5 %collective-permute-done.3 = bf16[256,512]{0,1:T(8,128)(2,1)S(1)} collective-permute-done((bf16[256,512]{0,1:T(8,128)(2,1)S(1)}, bf16[256,512]{0,1:T(8,128)(2,1)S(1)}, u32[]{:S(2)}, u32[]{:S(2)}) %collective-permute-start.3) | collective-permute-done | bytes 262176 | tf_op jit(solution)/shard_map/ppermute | solution.py:39
  36.8 8.5 %collective-permute-done.4 = bf16[256,512]{0,1:T(8,128)(2,1)S(1)} collective-permute-done((bf16[256,512]{0,1:T(8,128)(2,1)S(1)}, bf16[256,512]{0,1:T(8,128)(2,1)S(1)}, u32[]{:S(2)}, u32[]{:S(2)}) %collective-permute-start.4) | collective-permute-done | bytes 262176 | tf_op jit(solution)/shard_map/ppermute | solution.py:39
  45.3 8.5 %collective-permute-done.5 = bf16[256,512]{0,1:T(8,128)(2,1)S(1)} collective-permute-done((bf16[256,512]{0,1:T(8,128)(2,1)S(1)}, bf16[256,512]{0,1:T(8,128)(2,1)S(1)}, u32[]{:S(2)}, u32[]{:S(2)}) %collective-permute-start.5) | collective-permute-done | bytes 262176 | tf_op jit(solution)/shard_map/ppermute | solution.py:39
  53.8 8.5 %collective-permute-done.6 = bf16[256,512]{0,1:T(8,128)(2,1)S(1)} collective-permute-done((bf16[256,512]{0,1:T(8,128)(2,1)S(1)}, bf16[256,512]{0,1:T(8,128)(2,1)S(1)}, u32[]{:S(2)}, u32[]{:S(2)}) %collective-permute-start.6) | collective-permute-done | bytes 262176 | tf_op jit(solution)/shard_map/ppermute | solution.py:39
  62.2 8.5 %collective-permute-done.7 = bf16[256,512]{0,1:T(8,128)(2,1)S(1)} collective-permute-done((bf16[256,512]{0,1:T(8,128)(2,1)S(1)}, bf16[256,512]{0,1:T(8,128)(2,1)S(1)}, u32[]{:S(2)}, u32[]{:S(2)}) %collective-permute-start.7) | collective-permute-done | bytes 262176 | tf_op jit(solution)/shard_map/ppermute | solution.py:39
  70.7 8.5 %collective-permute-done.8 = bf16[256,512]{0,1:T(8,128)(2,1)S(1)} collective-permute-done((bf16[256,512]{0,1:T(8,128)(2,1)S(1)}, bf16[256,512]{0,1:T(8,128)(2,1)S(1)}, u32[]{:S(2)}, u32[]{:S(2)}) %collective-permute-start.8) | collective-permute-done | bytes 262176 | tf_op jit(solution)/shard_map/ppermute | solution.py:39
  79.2 8.5 %collective-permute-done.9 = bf16[256,512]{0,1:T(8,128)(2,1)S(1)} collective-permute-done((bf16[256,512]{0,1:T(8,128)(2,1)S(1)}, bf16[256,512]{0,1:T(8,128)(2,1)S(1)}, u32[]{:S(2)}, u32[]{:S(2)}) %collective-permute-start.9) | collective-permute-done | bytes 262176 | tf_op jit(solution)/shard_map/ppermute | solution.py:39
  87.7 8.5 %collective-permute-done.10 = bf16[256,512]{0,1:T(8,128)(2,1)S(1)} collective-permute-done((bf16[256,512]{0,1:T(8,128)(2,1)S(1)}, bf16[256,512]{0,1:T(8,128)(2,1)S(1)}, u32[]{:S(2)}, u32[]{:S(2)}) %collective-permute-start.10) | collective-permute-done | bytes 262176 | tf_op jit(solution)/shard_map/ppermute | solution.py:39
  96.2 8.5 %collective-permute-done.11 = bf16[256,512]{0,1:T(8,128)(2,1)S(1)} collective-permute-done((bf16[256,512]{0,1:T(8,128)(2,1)S(1)}, bf16[256,512]{0,1:T(8,128)(2,1)S(1)}, u32[]{:S(2)}, u32[]{:S(2)}) %collective-permute-start.11) | collective-permute-done | bytes 262176 | tf_op jit(solution)/shard_map/ppermute | solution.py:39
  104.7 8.5 %collective-permute-done.12 = bf16[256,512]{0,1:T(8,128)(2,1)S(1)} collective-permute-done((bf16[256,512]{0,1:T(8,128)(2,1)S(1)}, bf16[256,512]{0,1:T(8,128)(2,1)S(1)}, u32[]{:S(2)}, u32[]{:S(2)}) %collective-permute-start.12) | collective-permute-done | bytes 262176 | tf_op jit(solution)/shard_map/ppermute | solution.py:39
  113.9 8.6 %collective-permute-done.13 = bf16[256,512]{0,1:T(8,128)(2,1)} collective-permute-done((bf16[256,512]{0,1:T(8,128)(2,1)S(1)}, bf16[256,512]{0,1:T(8,128)(2,1)}, u32[]{:S(2)}, u32[]{:S(2)}) %collective-permute-start.13) | collective-permute-done | bytes 262176 | tf_op jit(solution)/shard_map/ppermute | solution.py:39
  122.5 8.8 %collective-permute-done.14 = bf16[256,512]{0,1:T(8,128)(2,1)} collective-permute-done((bf16[256,512]{0,1:T(8,128)(2,1)}, bf16[256,512]{0,1:T(8,128)(2,1)}, u32[]{:S(2)}, u32[]{:S(2)}) %collective-permute-start.14) | collective-permute-done | bytes 262176 | tf_op jit(solution)/shard_map/ppermute | solution.py:39
  139.2 5.6 %all-to-all-start = ((bf16[256,2,4096]{0,2,1:T(8,128)(2,1)}), bf16[256,2,4096]{0,2,1:T(8,128)(2,1)}, u32[]{:S(2)}, u32[]{:S(2)}) async-start(bf16[256,2,4096]{0,2,1:T(8,128)(2,1)} %bitcast.28), calls=%async_computation | async-start | bytes 8388608 | tf_op jit(solution)/shard_map/all_to_all | solution.py:43
  145.5 46.1 %all_gather.3 = bf16[512,512]{1,0:T(8,128)(2,1)S(1)} all-gather(bf16[256,512]{1,0:T(8,128)(2,1)S(1)} %copy-done.4), channel_id=1, replica_groups=mesh['col'=16,'tok'=2] {'tok'}, dimensions={0}, use_global_device_ids=true | all-gather | bytes 786432 | tf_op jit(solution)/shard_map/all_gather | solution.py:44
  191.6 6.3 %copy.20 = bf16[2,256,4096]{2,1,0:T(8,128)(2,1)} copy(bf16[2,256,4096]{1,2,0:T(8,128)(2,1)} %bitcast.1) | data formatting | bytes 8388608 | tf_op jit(solution)/shard_map/all_to_all | solution.py:43
  197.9 6.6 %convolution_convert_fusion = bf16[4096,512]{1,0:T(8,128)(2,1)} fusion(bf16[512,4096]{1,0:T(8,128)(2,1)} %bitcast.35, bf16[512,512]{1,0:T(8,128)(2,1)S(1)} %all_gather.3), kind=kOutput, calls=%fused_computation.6 | convolution fusion | flops 2149580800 | bytes 8912896 | tf_op jit(solution)/shard_map/dot_general | solution.py:45
  233.2 4.7 %constant_dynamic-update-slice_fusion.36 = bf16[4,1024,1024]{2,1,0:T(8,128)(2,1)} fusion(bf16[4,1024,1024]{2,1,0:T(8,128)(2,1)} %constant_dynamic-update-slice_fusion.37, bf16[4,512,1024]{2,1,0:T(8,128)(2,1)} %collective-permute-done.16, s32[]{:T(128)S(6)} %select_n.44), kind=kLoop, calls=%fused_computation.55 | loop fusion | bytes 8388612 | tf_op jit(solution)/shard_map/dynamic_update_slice | solution.py:27
  255.7 29.9 %constant_dynamic-update-slice_fusion.33 = (bf16[4,1024,1024]{2,1,0:T(8,128)(2,1)}, bf16[4,1024,512]{2,1,0:T(8,128)(2,1)}, f32[4,1024,512]{2,1,0:T(8,128)}, f32[4,1024,512]{2,1,0:T(8,128)}) fusion(bf16[4,1024,1024]{2,1,0:T(8,128)(2,1)} %broadcast.18, s32[]{:T(128)S(6)} %select_n.43, f32[4,1024,512]{2,1,0:T(8,128)} %bitcast.34, ...), kind=kOutput, calls=%fused_computation.51 | convolution fusion | flops 8613003264 | bytes 62914568 | tf_op jit(solution)/shard_map/nab,nac->nbc/dot_general | solution.py:65
  286.1 15.4 %multiply_add_fusion.2 = f32[4,512,1024]{2,1,0:T(8,128)} fusion(f32[4,512,1024]{2,1,0:T(8,128)} %param.10, bf16[4,1024,1024]{2,1,0:T(8,128)(2,1)} %constant_dynamic-update-slice_fusion.38, s32[]{:T(128)S(6)} %select_n.45), kind=kOutput, calls=%fused_computation.5 | convolution fusion | flops 4301258752 | bytes 29360132 | tf_op jit(solution)/shard_map/nab,ncb->nac/dot_general | solution.py:59
  301.5 15.3 %multiply_add_fusion.1 = f32[4,512,1024]{2,1,0:T(8,128)} fusion(f32[4,512,1024]{2,1,0:T(8,128)} %param.11, bf16[4,1024,512]{2,1,0:T(8,128)(2,1)} %bitcast.3, bf16[4,1024,1024]{2,1,0:T(8,128)(2,1)} %constant_dynamic-update-slice_fusion.38), kind=kOutput, calls=%fused_computation.4 | convolution fusion | flops 4301258752 | bytes 29360128 | tf_op jit(solution)/shard_map/nat,nab->ntb/dot_general | solution.py:62
  321.3 14.5 %fusion.13 = bf16[4,1024,512]{2,1,0:T(8,128)(2,1)} fusion(bf16[4,1024,1024]{2,1,0:T(8,128)(2,1)} %constant_dynamic-update-slice_fusion.36, bf16[4,1024,1024]{2,1,0:T(8,128)(2,1)} %constant_dynamic-update-slice_fusion.32, bf16[4,512,1024]{2,1,0:T(8,128)(2,1)} %param.13), kind=kOutput, calls=%fused_computation.17 | convolution fusion | flops 8592031744 | bytes 25165824 | tf_op jit(solution)/shard_map/nab,nbc->nac/dot_general | solution.py:81
  (90 shorter events, 62.1 us)
Async XLA Ops:
  1.7 9.6 %collective-permute-start = (bf16[256,512]{0,1:T(8,128)(2,1)S(1)}, bf16[256,512]{0,1:T(8,128)(2,1)S(1)}, u32[]{:S(2)}, u32[]{:S(2)}) collective-permute-start(bf16[256,512]{0,1:T(8,128)(2,1)S(1)} %copy.17), channel_id=1, source_target_pairs={{0,2},{2,4},{4,6},{6,8},{8,10},{10,12},{12,14},{14,16},{16,18},{18... | collective-permute-start | bytes 786440 | tf_op jit(solution)/shard_map/ppermute | solution.py:39
  11.3 8.5 %collective-permute-start.1 = (bf16[256,512]{0,1:T(8,128)(2,1)S(1)}, bf16[256,512]{0,1:T(8,128)(2,1)S(1)}, u32[]{:S(2)}, u32[]{:S(2)}) collective-permute-start(bf16[256,512]{0,1:T(8,128)(2,1)S(1)} %collective-permute-done), channel_id=1, source_target_pairs={{0,2},{2,4},{4,6},{6,8},{8,10},{10,12},{12,14},{14,16},{16,18},{18... | collective-permute-start | bytes 786440 | tf_op jit(solution)/shard_map/ppermute | solution.py:39
  19.8 8.5 %collective-permute-start.2 = (bf16[256,512]{0,1:T(8,128)(2,1)S(1)}, bf16[256,512]{0,1:T(8,128)(2,1)S(1)}, u32[]{:S(2)}, u32[]{:S(2)}) collective-permute-start(bf16[256,512]{0,1:T(8,128)(2,1)S(1)} %collective-permute-done.1), channel_id=1, source_target_pairs={{0,2},{2,4},{4,6},{6,8},{8,10},{10,12},{12,14},{14,16},{16,18},{18... | collective-permute-start | bytes 786440 | tf_op jit(solution)/shard_map/ppermute | solution.py:39
  28.3 8.5 %collective-permute-start.3 = (bf16[256,512]{0,1:T(8,128)(2,1)S(1)}, bf16[256,512]{0,1:T(8,128)(2,1)S(1)}, u32[]{:S(2)}, u32[]{:S(2)}) collective-permute-start(bf16[256,512]{0,1:T(8,128)(2,1)S(1)} %collective-permute-done.2), channel_id=1, source_target_pairs={{0,2},{2,4},{4,6},{6,8},{8,10},{10,12},{12,14},{14,16},{16,18},{18... | collective-permute-start | bytes 786440 | tf_op jit(solution)/shard_map/ppermute | solution.py:39
  36.8 8.5 %collective-permute-start.4 = (bf16[256,512]{0,1:T(8,128)(2,1)S(1)}, bf16[256,512]{0,1:T(8,128)(2,1)S(1)}, u32[]{:S(2)}, u32[]{:S(2)}) collective-permute-start(bf16[256,512]{0,1:T(8,128)(2,1)S(1)} %collective-permute-done.3), channel_id=1, source_target_pairs={{0,2},{2,4},{4,6},{6,8},{8,10},{10,12},{12,14},{14,16},{16,18},{18... | collective-permute-start | bytes 786440 | tf_op jit(solution)/shard_map/ppermute | solution.py:39
  45.3 8.5 %collective-permute-start.5 = (bf16[256,512]{0,1:T(8,128)(2,1)S(1)}, bf16[256,512]{0,1:T(8,128)(2,1)S(1)}, u32[]{:S(2)}, u32[]{:S(2)}) collective-permute-start(bf16[256,512]{0,1:T(8,128)(2,1)S(1)} %collective-permute-done.4), channel_id=1, source_target_pairs={{0,2},{2,4},{4,6},{6,8},{8,10},{10,12},{12,14},{14,16},{16,18},{18... | collective-permute-start | bytes 786440 | tf_op jit(solution)/shard_map/ppermute | solution.py:39
  53.7 8.5 %collective-permute-start.6 = (bf16[256,512]{0,1:T(8,128)(2,1)S(1)}, bf16[256,512]{0,1:T(8,128)(2,1)S(1)}, u32[]{:S(2)}, u32[]{:S(2)}) collective-permute-start(bf16[256,512]{0,1:T(8,128)(2,1)S(1)} %collective-permute-done.5), channel_id=1, source_target_pairs={{0,2},{2,4},{4,6},{6,8},{8,10},{10,12},{12,14},{14,16},{16,18},{18... | collective-permute-start | bytes 786440 | tf_op jit(solution)/shard_map/ppermute | solution.py:39
  62.2 8.5 %collective-permute-start.7 = (bf16[256,512]{0,1:T(8,128)(2,1)S(1)}, bf16[256,512]{0,1:T(8,128)(2,1)S(1)}, u32[]{:S(2)}, u32[]{:S(2)}) collective-permute-start(bf16[256,512]{0,1:T(8,128)(2,1)S(1)} %collective-permute-done.6), channel_id=1, source_target_pairs={{0,2},{2,4},{4,6},{6,8},{8,10},{10,12},{12,14},{14,16},{16,18},{18... | collective-permute-start | bytes 786440 | tf_op jit(solution)/shard_map/ppermute | solution.py:39
  70.7 8.5 %collective-permute-start.8 = (bf16[256,512]{0,1:T(8,128)(2,1)S(1)}, bf16[256,512]{0,1:T(8,128)(2,1)S(1)}, u32[]{:S(2)}, u32[]{:S(2)}) collective-permute-start(bf16[256,512]{0,1:T(8,128)(2,1)S(1)} %collective-permute-done.7), channel_id=1, source_target_pairs={{0,2},{2,4},{4,6},{6,8},{8,10},{10,12},{12,14},{14,16},{16,18},{18... | collective-permute-start | bytes 786440 | tf_op jit(solution)/shard_map/ppermute | solution.py:39
  79.2 8.5 %collective-permute-start.9 = (bf16[256,512]{0,1:T(8,128)(2,1)S(1)}, bf16[256,512]{0,1:T(8,128)(2,1)S(1)}, u32[]{:S(2)}, u32[]{:S(2)}) collective-permute-start(bf16[256,512]{0,1:T(8,128)(2,1)S(1)} %collective-permute-done.8), channel_id=1, source_target_pairs={{0,2},{2,4},{4,6},{6,8},{8,10},{10,12},{12,14},{14,16},{16,18},{18... | collective-permute-start | bytes 786440 | tf_op jit(solution)/shard_map/ppermute | solution.py:39
  87.7 8.5 %collective-permute-start.10 = (bf16[256,512]{0,1:T(8,128)(2,1)S(1)}, bf16[256,512]{0,1:T(8,128)(2,1)S(1)}, u32[]{:S(2)}, u32[]{:S(2)}) collective-permute-start(bf16[256,512]{0,1:T(8,128)(2,1)S(1)} %collective-permute-done.9), channel_id=1, source_target_pairs={{0,2},{2,4},{4,6},{6,8},{8,10},{10,12},{12,14},{14,16},{16,18},{18... | collective-permute-start | bytes 786440 | tf_op jit(solution)/shard_map/ppermute | solution.py:39
  96.2 8.5 %collective-permute-start.11 = (bf16[256,512]{0,1:T(8,128)(2,1)S(1)}, bf16[256,512]{0,1:T(8,128)(2,1)S(1)}, u32[]{:S(2)}, u32[]{:S(2)}) collective-permute-start(bf16[256,512]{0,1:T(8,128)(2,1)S(1)} %collective-permute-done.10), channel_id=1, source_target_pairs={{0,2},{2,4},{4,6},{6,8},{8,10},{10,12},{12,14},{14,16},{16,18},{18... | collective-permute-start | bytes 786440 | tf_op jit(solution)/shard_map/ppermute | solution.py:39
  104.7 8.5 %collective-permute-start.12 = (bf16[256,512]{0,1:T(8,128)(2,1)S(1)}, bf16[256,512]{0,1:T(8,128)(2,1)S(1)}, u32[]{:S(2)}, u32[]{:S(2)}) collective-permute-start(bf16[256,512]{0,1:T(8,128)(2,1)S(1)} %collective-permute-done.11), channel_id=1, source_target_pairs={{0,2},{2,4},{4,6},{6,8},{8,10},{10,12},{12,14},{14,16},{16,18},{18... | collective-permute-start | bytes 786440 | tf_op jit(solution)/shard_map/ppermute | solution.py:39
  113.9 8.6 %collective-permute-start.13 = (bf16[256,512]{0,1:T(8,128)(2,1)S(1)}, bf16[256,512]{0,1:T(8,128)(2,1)}, u32[]{:S(2)}, u32[]{:S(2)}) collective-permute-start(bf16[256,512]{0,1:T(8,128)(2,1)S(1)} %collective-permute-done.12), channel_id=1, source_target_pairs={{0,2},{2,4},{4,6},{6,8},{8,10},{10,12},{12,14},{14,16},{16,18},{18... | collective-permute-start | bytes 786440 | tf_op jit(solution)/shard_map/ppermute | solution.py:39
  122.5 8.8 %collective-permute-start.14 = (bf16[256,512]{0,1:T(8,128)(2,1)}, bf16[256,512]{0,1:T(8,128)(2,1)}, u32[]{:S(2)}, u32[]{:S(2)}) collective-permute-start(bf16[256,512]{0,1:T(8,128)(2,1)} %collective-permute-done.13), channel_id=1, source_target_pairs={{0,2},{2,4},{4,6},{6,8},{8,10},{10,12},{12,14},{14,16},{16,18},{18... | collective-permute-start | bytes 786440 | tf_op jit(solution)/shard_map/ppermute | solution.py:39
  122.5 14.0 %copy-start.3 = (bf16[256,512]{0,1:T(8,128)(2,1)S(1)}, bf16[256,512]{0,1:T(8,128)(2,1)}, u32[]{:S(2)}) copy-start(bf16[256,512]{0,1:T(8,128)(2,1)} %copy-done.2) | copy-start | bytes 786436
  136.9 8.5 %copy-start.4 = (bf16[256,512]{1,0:T(8,128)(2,1)S(1)}, bf16[256,512]{1,0:T(8,128)(2,1)}, u32[]{:S(2)}) copy-start(bf16[256,512]{1,0:T(8,128)(2,1)} %param.9) | copy-start | bytes 786436
  139.2 52.3 %all-to-all-start = ((bf16[256,2,4096]{0,2,1:T(8,128)(2,1)}), bf16[256,2,4096]{0,2,1:T(8,128)(2,1)}, u32[]{:S(2)}, u32[]{:S(2)}) async-start(bf16[256,2,4096]{0,2,1:T(8,128)(2,1)} %bitcast.28), calls=%async_computation | async-start | bytes 8388608 | tf_op jit(solution)/shard_map/all_to_all | solution.py:43
  144.9 83.7 %collective-permute-start.17 = (bf16[4,512,1024]{2,1,0:T(8,128)(2,1)}, bf16[4,512,1024]{2,1,0:T(8,128)(2,1)}, u32[]{:S(2)}, u32[]{:S(2)}) collective-permute-start(bf16[4,512,1024]{2,1,0:T(8,128)(2,1)} %param.13), channel_id=1, source_target_pairs={{0,2},{2,0},{4,6},{6,4},{8,10},{10,8},{12,14},{14,12},{16,18},{18,... | collective-permute-start | bytes 12582920 | tf_op jit(solution)/shard_map/ppermute | solution.py:16
  145.0 88.2 %collective-permute-start.16 = (bf16[4,512,1024]{2,1,0:T(8,128)(2,1)}, bf16[4,512,1024]{2,1,0:T(8,128)(2,1)}, u32[]{:S(2)}, u32[]{:S(2)}) collective-permute-start(bf16[4,512,1024]{2,1,0:T(8,128)(2,1)} %param.12), channel_id=1, source_target_pairs={{0,2},{2,0},{4,6},{6,4},{8,10},{10,8},{12,14},{14,12},{16,18},{18,... | collective-permute-start | bytes 12582920 | tf_op jit(solution)/shard_map/ppermute | solution.py:16
  204.5 42.4 %collective-permute-start.15 = (bf16[4,1024,512]{2,1,0:T(8,128)(2,1)}, bf16[4,1024,512]{2,1,0:T(8,128)(2,1)}, u32[]{:S(2)}, u32[]{:S(2)}) collective-permute-start(bf16[4,1024,512]{2,1,0:T(8,128)(2,1)} %bitcast.3), channel_id=1, source_target_pairs={{0,2},{2,0},{4,6},{6,4},{8,10},{10,8},{12,14},{14,12},{16,18},{18,... | collective-permute-start | bytes 12582920 | tf_op jit(solution)/shard_map/ppermute | solution.py:16
  211.5 6.9 %slice-start = ((s8[8388608]{0:T(1024)(128)(4,1)}), s8[4194304]{0:T(1024)(128)(4,1)S(1)}, s32[]{:S(2)}) async-start(s8[8388608]{0:T(1024)(128)(4,1)} %bitcast.29), calls=%async_computation.1 | async-start | bytes 8388608
  215.9 8.2 %slice-start.2 = ((s8[8388608]{0:T(1024)(128)(4,1)}), s8[4194304]{0:T(1024)(128)(4,1)S(1)}, s32[]{:S(2)}) async-start(s8[8388608]{0:T(1024)(128)(4,1)} %bitcast.31), calls=%async_computation.3 | async-start | bytes 8388608
  285.6 31.2 %collective-permute-start.18 = (bf16[4,1024,512]{2,1,0:T(8,128)(2,1)}, bf16[4,1024,512]{2,1,0:T(8,128)(2,1)}, u32[]{:S(2)}, u32[]{:S(2)}) collective-permute-start(bf16[4,1024,512]{2,1,0:T(8,128)(2,1)} %get-tuple-element.6), channel_id=1, source_target_pairs={{0,2},{2,0},{4,6},{6,4},{8,10},{10,8},{12,14},{14,12},{16,18},{18,... | collective-permute-start | bytes 12582920 | tf_op jit(solution)/shard_map/ppermute | solution.py:16
  (5 other events, 20.3 us)
